TPU v7x, 32 devices: a whole 2x2x4 slice. The times are simulated.
32 devices in a mesh: rep: 4 (over x, core), shard: 8 (over z, y).
Axes of the slice: x: 2, y: 2, z: 4, core: 2. Of those that a mesh axis runs over, the one named last changes fastest.
Arguments:
- inputs: bfloat16 [32, 1024, 512], P(('rep', 'shard')), may hold values from -6 to 6
- segments: int32 [32, 1024], P(('rep', 'shard')), may hold values from 0 to 7, never falling along the last dimension, each value on 1 to 512 neighbouring positions
- valid_mask: int32 [32, 1024], P(('rep', 'shard')), may hold values from 0 to 1, as said below
- teacher: bfloat16 [32, 1024, 512], P(('rep', 'shard')), may hold values from -6 to 6
- query_weight: bfloat16 [512, 512], P('shard'), may hold values from -0.5 to 0.5
- key_weight: bfloat16 [512, 512], P('shard'), may hold values from -0.25 to 0.25
- value_weight: bfloat16 [512, 512], P('shard'), may hold values from -0.25 to 0.25
- control_weight: bfloat16 [512, 512], P('shard'), may hold values from -0.75 to 0.75
- output_weight: bfloat16 [512, 512], P('shard'), may hold values from -0.75 to 0.75
- gain_first: bfloat16 [512], P('shard'), may hold values from 0.5 to 1.5
- shift_first: bfloat16 [512], P('shard'), may hold values from -4 to 4
- expand_weight: bfloat16 [512, 2048], P('shard'), may hold values from -0.25 to 0.25
- expand_bias: bfloat16 [2048], P('shard'), may hold values from -4 to 4
- contract_weight: bfloat16 [2048, 512], P('shard'), may hold values from -0.1875 to 0.1875
- contract_bias: bfloat16 [512], P('shard'), may hold values from -4 to 4
- gain_second: bfloat16 [512], P('shard'), may hold values from 0.5 to 1.5
- shift_second: bfloat16 [512], P('shard'), may hold values from -4 to 4
Outputs:
- layer_out: bfloat16 [32, 1024, 512], P(('rep', 'shard'))
- grad_inputs: float32 [32, 1024, 512], P(('rep', 'shard'))
- loss_value: float32 [], replicated
- grad_query_weight: float32 [512, 512], P('shard')
- grad_key_weight: float32 [512, 512], P('shard')
- grad_value_weight: float32 [512, 512], P('shard')
- grad_control_weight: float32 [512, 512], P('shard')
- grad_output_weight: float32 [512, 512], P('shard')
- grad_gain_first: float32 [512], P('shard')
- grad_shift_first: float32 [512], P('shard')
- grad_expand_weight: float32 [512, 2048], P('shard')
- grad_expand_bias: float32 [2048], P('shard')
- grad_contract_weight: float32 [2048, 512], P('shard')
- grad_contract_bias: float32 [512], P('shard')
- grad_gain_second: float32 [512], P('shard')
- grad_shift_second: float32 [512], P('shard')
Inputs may be any that keep to these rules, and one draw needn't show every extreme that they name: `valid_mask`: 1 marks a token that counts toward the loss; the first token of every sequence always counts. `segments`: within each sequence ids start at 0 and never fall; each document has 1 to 512 tokens, and one has exactly 512.
All inputs are finite; a program needn't handle non-finite values.
Results may differ from a plain program's by a relative error of at most 0.017.
Values may be sent and summed in bfloat16 or wider, within the bound.
No kernel may reach another device: no remote copies, remote signals or barrier semaphores. Data moves between devices by JAX's collectives and lax.ppermute only.
A program may use at most 128 MiB of HBM per device.

v0:
```python
from functools import partial
import jax
import jax.numpy as jnp
from jax import lax
from jax.sharding import PartitionSpec as P

HEADS = 8
EPSILON = 1e-05
HIGHEST = lax.Precision.HIGHEST
THREEPASS = lax.Precision.HIGH


def layer_norm(activations, gain, shift):
    row_mean = jnp.mean(activations, axis=-1, keepdims=True)
    centred = activations - row_mean
    variance = jnp.mean(centred * centred, axis=-1, keepdims=True)
    return centred * lax.rsqrt(variance + EPSILON) * gain + shift


def doc_mask(segment_row):
    places = jnp.arange(segment_row.shape[0], dtype=jnp.int32)
    earlier = places[None, :] <= places[:, None]
    same_document = segment_row[:, None] == segment_row[None, :]
    return jnp.where(earlier & same_document, 1.0, 0.0).astype(jnp.bfloat16)


def product(left, right):
    return jnp.dot(left, right, preferred_element_type=jnp.float32)


def head_scores(queries, key_rows):
    return product(queries, key_rows.T) * queries.shape[-1] ** (-0.5)


def slot_rest(causal, scores, value_rows, control):
    weights = jnp.exp(control)
    totals = jnp.dot(causal, weights, precision=THREEPASS, preferred_element_type=jnp.float32)
    slot_scores = jnp.dot(scores * causal, weights, precision=HIGHEST) / totals
    slot_shares = jax.nn.softmax(slot_scores, axis=-1)
    mixing = jnp.dot(slot_shares / totals, weights.T, precision=HIGHEST) * causal
    return jnp.dot(mixing, value_rows, precision=THREEPASS, preferred_element_type=jnp.float32)


def head_forward(causal, head_bundle):
    queries, key_rows, value_rows, control = head_bundle
    return slot_rest(causal, head_scores(queries, key_rows), value_rows, control)


def head_backward(causal, head_bundle):
    queries, key_rows, value_rows, control, grad_mixed = head_bundle
    scores = head_scores(queries, key_rows)
    outcome, pullback = jax.vjp(partial(slot_rest, causal), scores, value_rows, control)
    grad_scores, grad_values, grad_control = pullback(grad_mixed)
    scale = queries.shape[-1] ** (-0.5)
    grad_queries = (
        jnp.dot(grad_scores, key_rows, precision=THREEPASS, preferred_element_type=jnp.float32)
        * scale
    )
    grad_keys = (
        jnp.dot(grad_scores.T, queries, precision=THREEPASS, preferred_element_type=jnp.float32)
        * scale
    )
    return (grad_queries, grad_keys, grad_values.astype(jnp.float32), grad_control)


def mix_forward(bundle):
    queries, key_rows, value_rows, control, segment_row = bundle
    causal = doc_mask(segment_row)
    return lax.map(partial(head_forward, causal), (queries, key_rows, value_rows, control))


def mix_backward(bundle):
    queries, key_rows, value_rows, control, grad_mixed, segment_row = bundle
    causal = doc_mask(segment_row)
    return lax.map(
        partial(head_backward, causal), (queries, key_rows, value_rows, control, grad_mixed)
    )


def split_heads(matrix, sequence_count):
    return matrix.reshape(sequence_count, -1, HEADS, matrix.shape[1] // HEADS).transpose(0, 2, 1, 3)


def merge_heads(stacked):
    sequence_count, head_count, length, head_width = stacked.shape
    return stacked.transpose(0, 2, 1, 3).reshape(sequence_count * length, head_count * head_width)


def local(
    inputs,
    segments,
    valid_mask,
    teacher,
    query_weight,
    key_weight,
    value_weight,
    control_weight,
    output_weight,
    gain_first,
    shift_first,
    expand_weight,
    expand_bias,
    contract_weight,
    contract_bias,
    gain_second,
    shift_second,
):
    sequence_count, length, width = inputs.shape
    total_rows = sequence_count * length
    valid_rows = valid_mask.reshape(total_rows, 1).astype(jnp.float32)
    local_count = jnp.sum(valid_rows)
    count_all = lax.psum(local_count, ("rep", "shard"))
    mixer_set = (
        lax.all_gather(query_weight, "shard", axis=0, tiled=True),
        lax.all_gather(key_weight, "shard", axis=0, tiled=True),
        lax.all_gather(value_weight, "shard", axis=0, tiled=True),
        lax.all_gather(control_weight, "shard", axis=0, tiled=True),
        lax.all_gather(output_weight, "shard", axis=0, tiled=True),
        lax.all_gather(gain_first, "shard", axis=0, tiled=True),
        lax.all_gather(shift_first, "shard", axis=0, tiled=True),
    )
    query_full, key_full, value_full, control_full, out_full, gain_one, shift_one = mixer_set
    layer_in = inputs.reshape(total_rows, width).astype(jnp.float32)
    normed_one, first_back = jax.vjp(
        layer_norm, layer_in, gain_one.astype(jnp.float32), shift_one.astype(jnp.float32)
    )
    normed_one = normed_one.astype(jnp.bfloat16)
    queries = product(normed_one, query_full).astype(jnp.bfloat16)
    key_rows = product(normed_one, key_full).astype(jnp.bfloat16)
    value_rows = product(normed_one, value_full).astype(jnp.bfloat16)
    control = product(normed_one, control_full)
    head_queries = split_heads(queries, sequence_count)
    head_keys = split_heads(key_rows, sequence_count)
    head_values = split_heads(value_rows, sequence_count)
    head_control = split_heads(control, sequence_count)
    mixed = lax.map(mix_forward, (head_queries, head_keys, head_values, head_control, segments))
    mixed_low = merge_heads(mixed).astype(jnp.bfloat16)
    hidden_one = layer_in + product(mixed_low, out_full)
    branch_set = (
        lax.all_gather(expand_weight, "shard", axis=0, tiled=True),
        lax.all_gather(expand_bias, "shard", axis=0, tiled=True),
        lax.all_gather(contract_weight, "shard", axis=0, tiled=True),
        lax.all_gather(contract_bias, "shard", axis=0, tiled=True),
        lax.all_gather(gain_second, "shard", axis=0, tiled=True),
        lax.all_gather(shift_second, "shard", axis=0, tiled=True),
    )
    expand_full, expand_shift, contract_full, contract_shift, gain_two, shift_two = branch_set
    normed_two, second_back = jax.vjp(
        layer_norm, hidden_one, gain_two.astype(jnp.float32), shift_two.astype(jnp.float32)
    )
    normed_two = normed_two.astype(jnp.bfloat16)
    before_relu = product(normed_two, expand_full) + expand_shift.astype(jnp.float32)
    after_relu = jnp.maximum(before_relu, 0.0).astype(jnp.bfloat16)
    result = hidden_one + (product(after_relu, contract_full) + contract_shift.astype(jnp.float32))
    layer_out = result.astype(jnp.bfloat16).reshape(sequence_count, length, width)
    error = result - teacher.reshape(total_rows, width).astype(jnp.float32)
    local_loss = jnp.sum(valid_rows * error * error)
    loss_all = lax.psum(local_loss, ("rep", "shard"))
    loss_value = loss_all / (2.0 * count_all)
    total_tokens = total_rows * lax.axis_size("rep") * lax.axis_size("shard")
    grad_result = total_tokens / count_all * valid_rows * error
    branch_set = (
        lax.all_gather(expand_weight, "shard", axis=0, tiled=True),
        lax.all_gather(expand_bias, "shard", axis=0, tiled=True),
        lax.all_gather(contract_weight, "shard", axis=0, tiled=True),
        lax.all_gather(contract_bias, "shard", axis=0, tiled=True),
        lax.all_gather(gain_second, "shard", axis=0, tiled=True),
        lax.all_gather(shift_second, "shard", axis=0, tiled=True),
    )
    expand_full, expand_shift, contract_full, contract_shift, gain_two, shift_two = branch_set
    grad_second_low = grad_result.astype(jnp.bfloat16)
    grad_contract = product(after_relu.T, grad_second_low)
    grad_contract_shift = jnp.sum(grad_second_low.astype(jnp.float32), axis=0)
    grad_after = product(grad_second_low, contract_full.T)
    grad_before = jnp.where(before_relu > 0, grad_after, 0.0).astype(jnp.bfloat16)
    grad_expand = product(normed_two.T, grad_before)
    grad_expand_shift = jnp.sum(grad_before.astype(jnp.float32), axis=0)
    grad_normed_two = product(grad_before, expand_full.T)
    grad_hidden_part, grad_gain_two, grad_shift_two = second_back(grad_normed_two)
    grad_hidden = grad_result + grad_hidden_part
    mixer_set = (
        lax.all_gather(query_weight, "shard", axis=0, tiled=True),
        lax.all_gather(key_weight, "shard", axis=0, tiled=True),
        lax.all_gather(value_weight, "shard", axis=0, tiled=True),
        lax.all_gather(control_weight, "shard", axis=0, tiled=True),
        lax.all_gather(output_weight, "shard", axis=0, tiled=True),
        lax.all_gather(gain_first, "shard", axis=0, tiled=True),
        lax.all_gather(shift_first, "shard", axis=0, tiled=True),
    )
    query_full, key_full, value_full, control_full, out_full, gain_one, shift_one = mixer_set
    grad_mixer_low = grad_hidden.astype(jnp.bfloat16)
    grad_output = product(mixed_low.T, grad_mixer_low)
    grad_mixed = product(grad_mixer_low, out_full.T)
    head_grads = lax.map(
        mix_backward,
        (
            head_queries,
            head_keys,
            head_values,
            head_control,
            split_heads(grad_mixed, sequence_count),
            segments,
        ),
    )
    grad_queries = merge_heads(head_grads[0]).astype(jnp.bfloat16)
    grad_key_rows = merge_heads(head_grads[1]).astype(jnp.bfloat16)
    grad_value_rows = merge_heads(head_grads[2]).astype(jnp.bfloat16)
    grad_control = merge_heads(head_grads[3]).astype(jnp.bfloat16)
    grad_query = product(normed_one.T, grad_queries)
    grad_key = product(normed_one.T, grad_key_rows)
    grad_value = product(normed_one.T, grad_value_rows)
    grad_control_full = product(normed_one.T, grad_control)
    grad_normed_one = (
        product(grad_queries, query_full.T)
        + product(grad_key_rows, key_full.T)
        + product(grad_value_rows, value_full.T)
        + product(grad_control, control_full.T)
    )
    grad_layer_in, grad_gain_one, grad_shift_one = first_back(grad_normed_one)
    grad_inputs = (grad_hidden + grad_layer_in).reshape(sequence_count, length, width)
    branch_parts = (
        lax.psum_scatter(
            grad_expand.astype(jnp.bfloat16), "shard", scatter_dimension=0, tiled=True
        ).astype(jnp.float32),
        lax.psum_scatter(
            grad_expand_shift.astype(jnp.bfloat16), "shard", scatter_dimension=0, tiled=True
        ).astype(jnp.float32),
        lax.psum_scatter(
            grad_contract.astype(jnp.bfloat16), "shard", scatter_dimension=0, tiled=True
        ).astype(jnp.float32),
        lax.psum_scatter(
            grad_contract_shift.astype(jnp.bfloat16), "shard", scatter_dimension=0, tiled=True
        ).astype(jnp.float32),
        lax.psum_scatter(
            grad_gain_two.astype(jnp.bfloat16), "shard", scatter_dimension=0, tiled=True
        ).astype(jnp.float32),
        lax.psum_scatter(
            grad_shift_two.astype(jnp.bfloat16), "shard", scatter_dimension=0, tiled=True
        ).astype(jnp.float32),
    )
    mixer_parts = (
        lax.psum_scatter(
            grad_query.astype(jnp.bfloat16), "shard", scatter_dimension=0, tiled=True
        ).astype(jnp.float32),
        lax.psum_scatter(
            grad_key.astype(jnp.bfloat16), "shard", scatter_dimension=0, tiled=True
        ).astype(jnp.float32),
        lax.psum_scatter(
            grad_value.astype(jnp.bfloat16), "shard", scatter_dimension=0, tiled=True
        ).astype(jnp.float32),
        lax.psum_scatter(
            grad_control_full.astype(jnp.bfloat16), "shard", scatter_dimension=0, tiled=True
        ).astype(jnp.float32),
        lax.psum_scatter(
            grad_output.astype(jnp.bfloat16), "shard", scatter_dimension=0, tiled=True
        ).astype(jnp.float32),
        lax.psum_scatter(
            grad_gain_one.astype(jnp.bfloat16), "shard", scatter_dimension=0, tiled=True
        ).astype(jnp.float32),
        lax.psum_scatter(
            grad_shift_one.astype(jnp.bfloat16), "shard", scatter_dimension=0, tiled=True
        ).astype(jnp.float32),
    )
    (
        part_expand,
        part_expand_shift,
        part_contract,
        part_contract_shift,
        part_gain_two,
        part_shift_two,
    ) = branch_parts
    part_query, part_key, part_value, part_control, part_output, part_gain_one, part_shift_one = (
        mixer_parts
    )
    summed = (
        lax.psum(part_query.astype(jnp.bfloat16), "rep").astype(jnp.float32),
        lax.psum(part_key.astype(jnp.bfloat16), "rep").astype(jnp.float32),
        lax.psum(part_value.astype(jnp.bfloat16), "rep").astype(jnp.float32),
        lax.psum(part_control.astype(jnp.bfloat16), "rep").astype(jnp.float32),
        lax.psum(part_output.astype(jnp.bfloat16), "rep").astype(jnp.float32),
        lax.psum(part_gain_one.astype(jnp.bfloat16), "rep").astype(jnp.float32),
        lax.psum(part_shift_one.astype(jnp.bfloat16), "rep").astype(jnp.float32),
        lax.psum(part_expand.astype(jnp.bfloat16), "rep").astype(jnp.float32),
        lax.psum(part_expand_shift.astype(jnp.bfloat16), "rep").astype(jnp.float32),
        lax.psum(part_contract.astype(jnp.bfloat16), "rep").astype(jnp.float32),
        lax.psum(part_contract_shift.astype(jnp.bfloat16), "rep").astype(jnp.float32),
        lax.psum(part_gain_two.astype(jnp.bfloat16), "rep").astype(jnp.float32),
        lax.psum(part_shift_two.astype(jnp.bfloat16), "rep").astype(jnp.float32),
    )
    return (
        layer_out,
        grad_inputs,
        loss_value,
        summed[0],
        summed[1],
        summed[2],
        summed[3],
        summed[4],
        summed[5],
        summed[6],
        summed[7],
        summed[8],
        summed[9],
        summed[10],
        summed[11],
        summed[12],
    )


def solution(mesh):
    in_specs = (
        P(("rep", "shard"), None, None),
        P(("rep", "shard"), None),
        P(("rep", "shard"), None),
        P(("rep", "shard"), None, None),
        P("shard", None),
        P("shard", None),
        P("shard", None),
        P("shard", None),
        P("shard", None),
        P("shard"),
        P("shard"),
        P("shard", None),
        P("shard"),
        P("shard", None),
        P("shard"),
        P("shard"),
        P("shard"),
    )
    out_specs = (
        P(("rep", "shard"), None, None),
        P(("rep", "shard"), None, None),
        P(),
        P("shard", None),
        P("shard", None),
        P("shard", None),
        P("shard", None),
        P("shard", None),
        P("shard"),
        P("shard"),
        P("shard", None),
        P("shard"),
        P("shard", None),
        P("shard"),
        P("shard"),
        P("shard"),
    )
    return jax.shard_map(local, mesh=mesh, in_specs=in_specs, out_specs=out_specs, check_vma=False)
```

profile of v0, /device:TPU:0, one launch (start us, length us, event | category | flops | bytes accessed | tf_op | source)
XLA Modules:
  0.0 1280.8 jit_solution(18241503229063410139)
XLA Ops:
  15.0 23.7 %all-reduce.13 = (bf16[512]{0:T(512)(128)(2,1)S(1)}, bf16[512]{0:T(512)(128)(2,1)S(1)}, bf16[512]{0:T(512)(128)(2,1)S(1)}, bf16[512]{0:T(512)(128)(2,1)S(1)}, bf16[512]{0:T(512)(128)(2,1)S(1)}) all-reduce(bf16[512]{0:T(512)(128)(2,1)S(1)} %dynamic-update-slice.1, ...), channel_id=1, replica_groups=mesh['rep'=4,'shard'=8] {'shard'}, use_global_device_ids=true, to_apply=%add.1 | all-reduce | flops 2560 | bytes 10240
  38.7 33.0 %all_gather.48 = bf16[512,512]{1,0:T(8,128)(2,1)S(1)} all-gather(bf16[64,512]{1,0:T(8,128)(2,1)} %param.25), channel_id=1, replica_groups=mesh['rep'=4,'shard'=8] {'shard'}, dimensions={0}, use_global_device_ids=true | all-gather | bytes 589824 | tf_op jit(solution)/shard_map/all_gather | solution.py:114
  71.7 32.5 %all_gather.49 = bf16[512,512]{1,0:T(8,128)(2,1)S(1)} all-gather(bf16[64,512]{1,0:T(8,128)(2,1)} %param.26), channel_id=1, replica_groups=mesh['rep'=4,'shard'=8] {'shard'}, dimensions={0}, use_global_device_ids=true | all-gather | bytes 589824 | tf_op jit(solution)/shard_map/all_gather | solution.py:115
  104.3 32.6 %all_gather.51 = bf16[512,512]{1,0:T(8,128)(2,1)S(1)} all-gather(bf16[64,512]{1,0:T(8,128)(2,1)} %param.27), channel_id=1, replica_groups=mesh['rep'=4,'shard'=8] {'shard'}, dimensions={0}, use_global_device_ids=true | all-gather | bytes 589824 | tf_op jit(solution)/shard_map/all_gather | solution.py:116
  136.8 31.2 %all_gather.50 = bf16[512,512]{1,0:T(8,128)(2,1)S(1)} all-gather(bf16[64,512]{1,0:T(8,128)(2,1)S(1)} %copy-done.27), channel_id=1, replica_groups=mesh['rep'=4,'shard'=8] {'shard'}, dimensions={0}, use_global_device_ids=true | all-gather | bytes 589824 | tf_op jit(solution)/shard_map/all_gather | solution.py:117
  185.8 126.4 %while.48 = (s32[]{:T(128)}, bf16[8,1024,64]{1,2,0:T(8,128)(2,1)S(1)}, bf16[8,1024,64]{2,1,0:T(8,128)(2,1)}, bf16[8,1024,64]{2,1,0:T(8,128)(2,1)}, f32[8,1024,64...) while((s32[]{:T(128)}, bf16[8,1024,64]{1,2,0:T(8,128)(2,1)S(1)}, ...), condition=%wide.region_5.6_spmd.clone, body=%wide.region_2.5_spmd.clone.sunk | while | flops 2571565056 | bytes 21272672 | solution.py:69
  190.7 4.9 fusion.317
  206.5 4.9 fusion.317
  222.2 4.9 fusion.317
  238.0 4.9 fusion.317
  253.7 4.9 fusion.317
  269.4 4.9 fusion.317
  285.2 4.9 fusion.317
  300.9 4.9 fusion.317
  312.3 16.9 %all-gather = bf16[8,1,256]{2,1,0:T(2,128)(2,1)S(1)} all-gather(bf16[1,1,256]{2,1,0:T(2,128)(2,1)S(1)} %reshape.342), channel_id=1, replica_groups=mesh['rep'=4,'shard'=8] {'shard'}, dimensions={0}, use_global_device_ids=true | all-gather | bytes 4608 | tf_op jit(solution)/shard_map/all_gather | solution.py:141
  332.1 31.3 %all_gather.52 = bf16[512,512]{1,0:T(8,128)(2,1)S(1)} all-gather(bf16[64,512]{1,0:T(8,128)(2,1)S(1)} %copy-done.28), channel_id=1, replica_groups=mesh['rep'=4,'shard'=8] {'shard'}, dimensions={0}, use_global_device_ids=true | all-gather | bytes 589824 | tf_op jit(solution)/shard_map/all_gather | solution.py:118
  366.0 7.4 fusion.220
  373.4 8.4 fusion.205
  381.8 37.4 %all-reduce.11 = (f32[]{:T(128)}, f32[]{:T(128)}) all-reduce(f32[]{:T(128)} %convert_reduce_fusion.1, f32[]{:T(128)} %get-tuple-element.343), channel_id=1, replica_groups=mesh['rep'=4,'shard'=8] {'rep','shard'}, use_global_device_ids=true, to_apply=%region_9.10 | all-reduce | flops 2 | bytes 16 | tf_op jit(solution)/shard_map/psum | solution.py:112
  422.7 6.9 fusion.235
  429.6 4.2 fusion.236
  458.0 363.5 %while.49 = (s32[]{:T(128)}, bf16[8,1024,64]{1,2,0:T(8,128)(2,1)}, bf16[8,1024,64]{1,2,0:T(8,128)(2,1)}, bf16[8,1024,64]{1,2,0:T(8,128)(2,1)}, bf16[8,1024,64]{1...) while((s32[]{:T(128)}, bf16[8,1024,64]{1,2,0:T(8,128)(2,1)}, ...), condition=%wide.region_16.17_spmd.clone, body=%wide.region_12.16_spmd.clone.sunk | while | flops 7448756224 | bytes 66475184 | solution.py:75
  483.8 4.8 fusion.336
  488.7 4.7 multiply_reduce_fusion.5
  525.7 4.8 fusion.336
  530.6 4.7 multiply_reduce_fusion.5
  567.5 4.8 fusion.336
  572.5 4.7 multiply_reduce_fusion.5
  609.4 4.8 fusion.336
  614.3 4.7 multiply_reduce_fusion.5
  651.3 4.8 fusion.336
  656.2 4.7 multiply_reduce_fusion.5
  693.2 4.8 fusion.336
  698.1 4.7 multiply_reduce_fusion.5
  735.0 4.8 fusion.336
  740.0 4.7 multiply_reduce_fusion.5
  776.9 4.8 fusion.336
  781.9 4.7 multiply_reduce_fusion.5
  833.1 7.4 convolution_convert_fusion
  841.1 6.0 convolution_convert_fusion.1
  856.8 31.3 %reduce-scatter.8.cloned.1.call-done = bf16[64,512]{1,0:T(8,128)(2,1)} async-done(((bf16[512,512]{1,0:T(8,128)(2,1)}), bf16[64,512]{1,0:T(8,128)(2,1)}) %reduce-scatter.8.cloned.1.call-update) | async-done | bytes 65552 | tf_op jit(solution)/shard_map/reduce_scatter | solution.py:242
  888.0 64.2 %reduce-scatter.14.cloned.1.call-done = bf16[64,512]{1,0:T(8,128)(2,1)} async-done(((bf16[512,512]{1,0:T(8,128)(2,1)}), bf16[64,512]{1,0:T(8,128)(2,1)}) %reduce-scatter.14.cloned.1.call-update) | async-done | bytes 65552 | tf_op jit(solution)/shard_map/reduce_scatter | solution.py:251
  952.2 64.5 %reduce-scatter.10.cloned.1.call-done = bf16[64,512]{1,0:T(8,128)(2,1)} async-done(((bf16[512,512]{1,0:T(8,128)(2,1)}), bf16[64,512]{1,0:T(8,128)(2,1)}) %reduce-scatter.10.cloned.1.call-update) | async-done | bytes 65552 | tf_op jit(solution)/shard_map/reduce_scatter | solution.py:245
  1016.7 64.3 %reduce-scatter.12.cloned.1.call-done = bf16[64,512]{1,0:T(8,128)(2,1)} async-done(((bf16[512,512]{1,0:T(8,128)(2,1)}), bf16[64,512]{1,0:T(8,128)(2,1)}) %reduce-scatter.12.cloned.1.call-update) | async-done | bytes 65552 | tf_op jit(solution)/shard_map/reduce_scatter | solution.py:248
  1081.0 70.8 %reduce-scatter.20.cloned.1.call-done = bf16[256,512]{1,0:T(8,128)(2,1)} async-done(((bf16[2048,512]{1,0:T(8,128)(2,1)}), bf16[256,512]{1,0:T(8,128)(2,1)}) %reduce-scatter.20.cloned.1.call-update) | async-done | bytes 262160 | tf_op jit(solution)/shard_map/reduce_scatter | solution.py:228
  1151.8 70.7 %reduce-scatter.18.cloned.1.call-done = bf16[64,2048]{1,0:T(8,128)(2,1)} async-done(((bf16[512,2048]{1,0:T(8,128)(2,1)}), bf16[64,2048]{1,0:T(8,128)(2,1)}) %reduce-scatter.18.cloned.1.call-update) | async-done | bytes 262160 | tf_op jit(solution)/shard_map/reduce_scatter | solution.py:222
  1225.5 19.6 %all-reduce.12 = (bf16[512]{0:T(512)(128)(2,1)S(1)}, bf16[512]{0:T(512)(128)(2,1)S(1)}, bf16[2048]{0:T(1024)(128)(2,1)S(1)}, bf16[512]{0:T(512)(128)(2,1)S(1)}, ...) all-reduce(bf16[512]{0:T(512)(128)(2,1)S(1)} %get-tuple-element.262, ...), channel_id=7, replica_groups=mesh['rep'=4,'shard'=8] {'shard'}, use_global_device_ids=true, to_apply=%region_32.33.clone | all-reduce | flops 4608 | bytes 18432
  1245.6 5.6 all-reduce.14
  (399 shorter events, 444.1 us)
Async XLA Ops:
  7.2 129.6 %copy-start.27 = (bf16[64,512]{1,0:T(8,128)(2,1)S(1)}, bf16[64,512]{1,0:T(8,128)(2,1)}, u32[]{:S(2)}) copy-start(bf16[64,512]{1,0:T(8,128)(2,1)} %param.28) | copy-start | bytes 196612
  7.2 358.8 %all-gather.4.cloned.1.call-start = ((), (), s32[]{:S(2)}) async-start(), calls=%async_computation.7 | async-start | bytes 2359296 | tf_op jit(solution)/shard_map/all_gather | solution.py:140
  7.9 365.5 %all-gather.6.cloned.1.call-start = ((), (), s32[]{:S(2)}) async-start(), calls=%async_computation.8 | async-start | bytes 2359296 | tf_op jit(solution)/shard_map/all_gather | solution.py:142
  8.7 848.1 %reduce-scatter.16.cloned.1.call-start = ((), (), s32[]{:S(2)}) async-start(), calls=%async_computation.13 | async-start | bytes 589824 | tf_op jit(solution)/shard_map/reduce_scatter | solution.py:254
  38.7 144.7 %copy-start.39 = (f32[512]{0:T(512)}, f32[512]{0:T(512)S(1)}, u32[]{:S(2)}) copy-start(f32[512]{0:T(512)S(1)} %convert_element_type.286) | copy-start | bytes 6148
  38.7 144.7 %copy-start.33 = (f32[512]{0:T(512)}, f32[512]{0:T(512)S(1)}, u32[]{:S(2)}) copy-start(f32[512]{0:T(512)S(1)} %convert_element_type.285) | copy-start | bytes 6148
  71.7 109.0 %copy-start.23 = (bf16[512,512]{1,0:T(8,128)(2,1)}, bf16[512,512]{1,0:T(8,128)(2,1)S(1)}, u32[]{:S(2)}) copy-start(bf16[512,512]{1,0:T(8,128)(2,1)S(1)} %all_gather.48) | copy-start | bytes 1572868
  104.2 67.4 %copy-start.19 = (bf16[512,512]{1,0:T(8,128)(2,1)}, bf16[512,512]{1,0:T(8,128)(2,1)S(1)}, u32[]{:S(2)}) copy-start(bf16[512,512]{1,0:T(8,128)(2,1)S(1)} %all_gather.49) | copy-start | bytes 1572868
  136.8 39.4 %copy-start.21 = (bf16[512,512]{1,0:T(8,128)(2,1)}, bf16[512,512]{1,0:T(8,128)(2,1)S(1)}, u32[]{:S(2)}) copy-start(bf16[512,512]{1,0:T(8,128)(2,1)S(1)} %all_gather.51) | copy-start | bytes 1572868
  170.5 192.9 %copy-start = (bf16[1,1024,512]{1,2,0:T(8,128)(2,1)}, bf16[1,1024,512]{1,2,0:T(8,128)(2,1)S(1)}, u32[]{:S(2)}) copy-start(bf16[1,1024,512]{1,2,0:T(8,128)(2,1)S(1)} %copy.51) | copy-start | bytes 3145732
  170.7 12.7 copy-start.25
  171.6 11.8 copy-start.29
  183.4 2.3 copy-start.46
  185.8 126.4 %copy-start.47 = (bf16[256]{0:T(256)(128)(2,1)S(1)}, bf16[256]{0:T(256)(128)(2,1)}, u32[]{:S(2)}) copy-start(bf16[256]{0:T(256)(128)(2,1)} %param.33) | copy-start | bytes 1540
  185.8 126.5 %copy-start.35 = (s32[1,1024]{1,0:T(1,128)S(1)}, s32[1,1024]{1,0:T(1,128)}, u32[]{:S(2)}) copy-start(s32[1,1024]{1,0:T(1,128)} %param.23) | copy-start | bytes 12292
  312.2 51.2 %copy-start.6 = (bf16[8,1024,64]{1,2,0:T(8,128)(2,1)}, bf16[8,1024,64]{1,2,0:T(8,128)(2,1)S(1)}, u32[]{:S(2)}) copy-start(bf16[8,1024,64]{1,2,0:T(8,128)(2,1)S(1)} %get-tuple-element.167) | copy-start | bytes 3145732
  312.2 19.9 %copy-start.28 = (bf16[64,512]{1,0:T(8,128)(2,1)S(1)}, bf16[64,512]{1,0:T(8,128)(2,1)}, u32[]{:S(2)}) copy-start(bf16[64,512]{1,0:T(8,128)(2,1)} %param.29) | copy-start | bytes 196612
  312.2 53.7 %copy-start.41 = (f32[512]{0:T(512)}, f32[512]{0:T(512)S(1)}, u32[]{:S(2)}) copy-start(f32[512]{0:T(512)S(1)} %convert_element_type.298) | copy-start | bytes 6148
  363.4 2.2 copy-start.14
  365.9 7.5 copy-start.8
  420.0 2.7 copy-start.45
  422.7 7.0 copy-start.24
  422.7 7.0 copy-start.44
  429.6 4.2 copy-start.48
  436.8 2.2 copy-start.4
  439.0 1.9 copy-start.10
  440.9 3.3 copy-start.7
  449.7 438.3 %reduce-scatter.8.cloned.1.call-start = ((), (), s32[]{:S(2)}) async-start(), calls=%async_computation.9 | async-start | bytes 589824 | tf_op jit(solution)/shard_map/reduce_scatter | solution.py:242
  458.0 363.6 %copy-start.1 = (bf16[1,1024,512]{1,2,0:T(8,128)(2,1)S(1)}, bf16[1,1024,512]{1,2,0:T(8,128)(2,1)}, u32[]{:S(2)}) copy-start(bf16[1,1024,512]{1,2,0:T(8,128)(2,1)} %copy-done) | copy-start | bytes 3145732
  458.0 363.6 %copy-start.26 = (f32[1024]{0:T(1024)S(1)}, f32[1024]{0:T(1024)}, u32[]{:S(2)}) copy-start(f32[1024]{0:T(1024)} %copy-done.25) | copy-start | bytes 12292
  458.0 363.6 %copy-start.30 = (f32[1024]{0:T(1024)S(1)}, f32[1024]{0:T(1024)}, u32[]{:S(2)}) copy-start(f32[1024]{0:T(1024)} %copy-done.29) | copy-start | bytes 12292
  458.0 363.6 %copy-start.34 = (f32[512]{0:T(512)S(1)}, f32[512]{0:T(512)}, u32[]{:S(2)}) copy-start(f32[512]{0:T(512)} %copy-done.33) | copy-start | bytes 6148
  458.0 363.6 %copy-start.40 = (f32[512]{0:T(512)S(1)}, f32[512]{0:T(512)}, u32[]{:S(2)}) copy-start(f32[512]{0:T(512)} %copy-done.39) | copy-start | bytes 6148
  481.8 1.9 copy-start.11
  607.5 1.9 copy-start.11
  733.1 1.9 copy-start.11
  824.4 127.8 %reduce-scatter.14.cloned.1.call-start = ((), (), s32[]{:S(2)}) async-start(), calls=%async_computation.12 | async-start | bytes 589824 | tf_op jit(solution)/shard_map/reduce_scatter | solution.py:251
  827.3 189.4 %reduce-scatter.10.cloned.1.call-start = ((), (), s32[]{:S(2)}) async-start(), calls=%async_computation.10 | async-start | bytes 589824 | tf_op jit(solution)/shard_map/reduce_scatter | solution.py:245
  830.2 250.8 %reduce-scatter.12.cloned.1.call-start = ((), (), s32[]{:S(2)}) async-start(), calls=%async_computation.11 | async-start | bytes 589824 | tf_op jit(solution)/shard_map/reduce_scatter | solution.py:248
  833.1 318.7 %reduce-scatter.20.cloned.1.call-start = ((), (), s32[]{:S(2)}) async-start(), calls=%async_computation.15 | async-start | bytes 2359296 | tf_op jit(solution)/shard_map/reduce_scatter | solution.py:228
  840.5 382.0 %reduce-scatter.18.cloned.1.call-start = ((), (), s32[]{:S(2)}) async-start(), calls=%async_computation.14 | async-start | bytes 2359296 | tf_op jit(solution)/shard_map/reduce_scatter | solution.py:222
  847.2 3.3 copy-start.15
  847.2 414.3 %all-reduce.18.cloned.1.call-start = ((), (), s32[]{:S(2)}) async-start(), calls=%async_computation.16 | async-start | bytes 1703936 | tf_op jit(solution)/shard_map/psum | solution.py:276
  856.7 368.8 %copy-start.36 = (bf16[512]{0:T(512)(128)(2,1)S(1)}, bf16[512]{0:T(512)(128)(2,1)}, u32[]{:S(2)}) copy-start(bf16[512]{0:T(512)(128)(2,1)} %get-tuple-element.260) | copy-start | bytes 3076
  856.7 368.8 %copy-start.37 = (bf16[2048]{0:T(1024)(128)(2,1)S(1)}, bf16[2048]{0:T(1024)(128)(2,1)}, u32[]{:S(2)}) copy-start(bf16[2048]{0:T(1024)(128)(2,1)} %get-tuple-element.346) | copy-start | bytes 12292
  856.7 368.8 %copy-start.38 = (bf16[512]{0:T(512)(128)(2,1)S(1)}, bf16[512]{0:T(512)(128)(2,1)}, u32[]{:S(2)}) copy-start(bf16[512]{0:T(512)(128)(2,1)} %get-tuple-element.330) | copy-start | bytes 3076
  856.7 368.8 %copy-start.43 = (bf16[512]{0:T(512)(128)(2,1)S(1)}, bf16[512]{0:T(512)(128)(2,1)}, u32[]{:S(2)}) copy-start(bf16[512]{0:T(512)(128)(2,1)} %get-tuple-element.348) | copy-start | bytes 3076
  856.7 397.6 %copy-start.3 = (f32[1024,512]{0,1:T(8,128)S(1)}, f32[1024,512]{0,1:T(8,128)}, u32[]{:S(2)}) copy-start(f32[1024,512]{0,1:T(8,128)} %copy-done.2) | copy-start | bytes 6291460
  (18 other events, 25.2 us)
Sparse Core Ops, SparseCore 0:
  10.1 59.2 all-gather.3
  71.6 55.8 all-gather.5
  449.8 63.3 reduce-scatter.15
  824.5 63.4 reduce-scatter.7
  891.2 60.9 reduce-scatter.13
  955.7 60.9 reduce-scatter.9
  1020.0 60.8 reduce-scatter.11
  1084.9 66.8 reduce-scatter.19
  1155.7 66.7 reduce-scatter.17
  1225.5 34.6 all-reduce.17
where the time goes:
time: 1290 us; the launch traced here: 1280 us
  matrix products  519 us (40%)
  waiting for transfers between devices  367 us (28%)
  blocking collectives  264 us (20%)
  local copies, waits for them, and re-layouts  49.7 us (4%)
  other arithmetic  30.4 us (2%)
  loops' own time  30.1 us (2%)
  between operations  20.2 us (2%)
    dot_general x32, matrix products, slot_rest(): slot_scores = jnp.dot(scores * causal, weights, precision=HIGHEST) / totals  134 us
    dot_general x32, matrix products, slot_rest(): jnp.dot(slot_shares / totals, weights.T, precision=HIGHEST) * causal  127 us
    dot_general x37, matrix products, product(): return jnp.dot(left, right, preferred_element_type=jnp.float32)  99.4 us
    reduce_scatter x1, waiting for transfers between devices, local(): lax.psum_scatter(grad_contract.astype(jnp.bfloat16), 'shard', scatter_dim...  70.8 us
    reduce_scatter x1, waiting for transfers between devices, local(): lax.psum_scatter(grad_expand.astype(jnp.bfloat16), 'shard', scatter_dimen...  70.7 us
    dot_general x24, matrix products, slot_rest(): jnp.dot(mixing, value_rows, precision=THREEPASS, preferred_element_type=j...  69.2 us
    reduce_scatter x1, waiting for transfers between devices, local(): lax.psum_scatter(grad_key.astype(jnp.bfloat16), 'shard', scatter_dimensio...  64.5 us
    reduce_scatter x1, waiting for transfers between devices, local(): lax.psum_scatter(grad_value.astype(jnp.bfloat16), 'shard', scatter_dimens...  64.3 us
  transfers between devices with their start and end apart: 10, of which 6 were waited for; matrix products, arithmetic and copies ran while one was open for 43% of the time, Pallas kernels for 0%

commit v1 on v0

--- a/solution.py
+++ b/solution.py
@@ -8,6 +8,19 @@
 EPSILON = 1e-05
 HIGHEST = lax.Precision.HIGHEST
 THREEPASS = lax.Precision.HIGH
+
+
+def gather_around(x, axis, dim):
+    ways = lax.axis_size(axis)
+    up = [(d, (d + 1) % ways) for d in range(ways)]
+    down = [(d, (d - 1) % ways) for d in range(ways)]
+    earlier, later = ([x], [x])
+    for _ in range(ways // 2):
+        earlier.append(lax.ppermute(earlier[-1], axis, up))
+    for _ in range((ways - 1) // 2):
+        later.append(lax.ppermute(later[-1], axis, down))
+    line = jnp.concatenate([*earlier[::-1], *later[1:]], axis=dim)
+    return jnp.roll(line, (lax.axis_index(axis) - ways // 2) * x.shape[dim], axis=dim)
 
 
 def layer_norm(activations, gain, shift):
@@ -115,7 +128,7 @@
         lax.all_gather(key_weight, "shard", axis=0, tiled=True),
         lax.all_gather(value_weight, "shard", axis=0, tiled=True),
         lax.all_gather(control_weight, "shard", axis=0, tiled=True),
-        lax.all_gather(output_weight, "shard", axis=0, tiled=True),
+        gather_around(output_weight, "shard", 0),
         lax.all_gather(gain_first, "shard", axis=0, tiled=True),
         lax.all_gather(shift_first, "shard", axis=0, tiled=True),
     )

time: 1290 us -> 1310 us (1.016)
  transfers between devices with their start and end apart: 10 -> 17, of which waited for: 6 -> 9; matrix products, arithmetic and copies ran while one was open for 43% -> 42% of each run, Pallas kernels for 0% -> 0%
where the time goes in v1:
time: 1310 us; the launch traced here: 1300 us
  matrix products  520 us (40%)
  waiting for transfers between devices  369 us (28%)
  blocking collectives  271 us (21%)
  local copies, waits for them, and re-layouts  48.7 us (4%)
  other arithmetic  30.4 us (2%)
  loops' own time  29.7 us (2%)
  between operations  20.3 us (2%)
    dot_general x32, matrix products, slot_rest(): slot_scores = jnp.dot(scores * causal, weights, precision=HIGHEST) / totals  134 us
    dot_general x32, matrix products, slot_rest(): jnp.dot(slot_shares / totals, weights.T, precision=HIGHEST) * causal  127 us
    dot_general x37, matrix products, product(): return jnp.dot(left, right, preferred_element_type=jnp.float32)  99.9 us
    reduce_scatter x1, waiting for transfers between devices, local(): lax.psum_scatter(grad_contract.astype(jnp.bfloat16), 'shard', scatter_dim...  70.6 us
    reduce_scatter x1, waiting for transfers between devices, local(): lax.psum_scatter(grad_expand.astype(jnp.bfloat16), 'shard', scatter_dimen...  70.6 us
    dot_general x24, matrix products, slot_rest(): jnp.dot(mixing, value_rows, precision=THREEPASS, preferred_element_type=j...  69.2 us
    reduce_scatter x1, waiting for transfers between devices, local(): lax.psum_scatter(grad_key.astype(jnp.bfloat16), 'shard', scatter_dimensio...  64.5 us
    reduce_scatter x1, waiting for transfers between devices, local(): lax.psum_scatter(grad_value.astype(jnp.bfloat16), 'shard', scatter_dimens...  64.3 us
  transfers between devices with their start and end apart: 17, of which 9 were waited for; matrix products, arithmetic and copies ran while one was open for 42% of the time, Pallas kernels for 0%

profile of v1, /device:TPU:0, one launch (start us, length us, event | category | flops | bytes accessed | tf_op | source)
XLA Modules:
  0.0 1301.4 jit_solution(3576006452956139288)
XLA Ops:
  8.0 6.1 collective-permute-start.4
  20.4 22.2 %all-reduce.13 = (bf16[512]{0:T(512)(128)(2,1)S(1)}, bf16[512]{0:T(512)(128)(2,1)S(1)}, bf16[512]{0:T(512)(128)(2,1)S(1)}, bf16[512]{0:T(512)(128)(2,1)S(1)}, bf16[512]{0:T(512)(128)(2,1)S(1)}) all-reduce(bf16[512]{0:T(512)(128)(2,1)S(1)} %dynamic-update-slice.1, ...), channel_id=1, replica_groups=mesh['rep'=4,'shard'=8] {'shard'}, use_global_device_ids=true, to_apply=%add.1 | all-reduce | flops 2560 | bytes 10240
  42.6 32.8 %all_gather.47 = bf16[512,512]{1,0:T(8,128)(2,1)S(1)} all-gather(bf16[64,512]{1,0:T(8,128)(2,1)} %param.25), channel_id=1, replica_groups=mesh['rep'=4,'shard'=8] {'shard'}, dimensions={0}, use_global_device_ids=true | all-gather | bytes 589824 | tf_op jit(solution)/shard_map/all_gather | solution.py:127
  75.4 33.2 %all_gather.48 = bf16[512,512]{1,0:T(8,128)(2,1)S(1)} all-gather(bf16[64,512]{1,0:T(8,128)(2,1)} %param.26), channel_id=1, replica_groups=mesh['rep'=4,'shard'=8] {'shard'}, dimensions={0}, use_global_device_ids=true | all-gather | bytes 589824 | tf_op jit(solution)/shard_map/all_gather | solution.py:128
  108.6 32.3 %all_gather.50 = bf16[512,512]{1,0:T(8,128)(2,1)S(1)} all-gather(bf16[64,512]{1,0:T(8,128)(2,1)} %param.27), channel_id=1, replica_groups=mesh['rep'=4,'shard'=8] {'shard'}, dimensions={0}, use_global_device_ids=true | all-gather | bytes 589824 | tf_op jit(solution)/shard_map/all_gather | solution.py:129
  140.8 31.2 %all_gather.49 = bf16[512,512]{1,0:T(8,128)(2,1)S(1)} all-gather(bf16[64,512]{1,0:T(8,128)(2,1)S(1)} %copy-done.29), channel_id=1, replica_groups=mesh['rep'=4,'shard'=8] {'shard'}, dimensions={0}, use_global_device_ids=true | all-gather | bytes 589824 | tf_op jit(solution)/shard_map/all_gather | solution.py:130
  190.4 126.0 %while.48 = (s32[]{:T(128)}, bf16[8,1024,64]{1,2,0:T(8,128)(2,1)S(1)}, bf16[8,1024,64]{2,1,0:T(8,128)(2,1)}, bf16[8,1024,64]{2,1,0:T(8,128)(2,1)}, f32[8,1024,64...) while((s32[]{:T(128)}, bf16[8,1024,64]{1,2,0:T(8,128)(2,1)S(1)}, ...), condition=%wide.region_5.6_spmd.clone, body=%wide.region_2.5_spmd.clone.sunk | while | flops 2571565056 | bytes 21272672 | solution.py:82
  194.9 5.0 fusion.318
  210.6 5.0 fusion.318
  226.4 5.0 fusion.318
  242.1 5.0 fusion.318
  257.9 5.0 fusion.318
  273.6 5.0 fusion.318
  289.4 5.0 fusion.318
  305.1 5.0 fusion.318
  317.0 34.6 %all_gather.57 = bf16[512,512]{1,0:T(8,128)(2,1)} all-gather(bf16[64,512]{1,0:T(8,128)(2,1)S(1)} %copy-done.26), channel_id=1, replica_groups=mesh['rep'=4,'shard'=8] {'shard'}, dimensions={0}, use_global_device_ids=true | all-gather | bytes 589824 | tf_op jit(solution)/shard_map/all_gather | solution.py:199
  351.7 19.0 %all-gather = bf16[8,1,256]{2,1,0:T(2,128)(2,1)S(1)} all-gather(bf16[1,1,256]{2,1,0:T(2,128)(2,1)S(1)} %reshape.342), channel_id=1, replica_groups=mesh['rep'=4,'shard'=8] {'shard'}, dimensions={0}, use_global_device_ids=true | all-gather | bytes 4608 | tf_op jit(solution)/shard_map/all_gather | solution.py:154
  384.5 7.4 fusion.222
  392.0 8.4 fusion.205
  400.4 40.7 %all-reduce.11 = (f32[]{:T(128)}, f32[]{:T(128)}) all-reduce(f32[]{:T(128)} %convert_reduce_fusion.1, f32[]{:T(128)} %get-tuple-element.343), channel_id=1, replica_groups=mesh['rep'=4,'shard'=8] {'rep','shard'}, use_global_device_ids=true, to_apply=%region_9.10 | all-reduce | flops 2 | bytes 16 | tf_op jit(solution)/shard_map/psum | solution.py:125
  444.5 6.9 fusion.237
  479.3 363.8 %while.49 = (s32[]{:T(128)}, bf16[8,1024,64]{1,2,0:T(8,128)(2,1)}, bf16[8,1024,64]{1,2,0:T(8,128)(2,1)}, bf16[8,1024,64]{1,2,0:T(8,128)(2,1)}, bf16[8,1024,64]{1...) while((s32[]{:T(128)}, bf16[8,1024,64]{1,2,0:T(8,128)(2,1)}, ...), condition=%wide.region_16.17_spmd.clone, body=%wide.region_12.16_spmd.clone.sunk | while | flops 7448756224 | bytes 66475184 | solution.py:88
  505.1 4.8 fusion.337
  510.0 4.8 multiply_reduce_fusion.5
  547.0 4.8 fusion.337
  551.9 4.8 multiply_reduce_fusion.5
  588.9 4.8 fusion.337
  593.8 4.8 multiply_reduce_fusion.5
  630.8 4.8 fusion.337
  635.7 4.8 multiply_reduce_fusion.5
  672.7 4.8 fusion.337
  677.6 4.8 multiply_reduce_fusion.5
  714.6 4.8 fusion.337
  719.6 4.8 multiply_reduce_fusion.5
  756.5 4.8 fusion.337
  761.5 4.8 multiply_reduce_fusion.5
  798.4 4.8 fusion.337
  803.4 4.8 multiply_reduce_fusion.5
  854.7 7.4 convolution_convert_fusion
  862.7 6.0 convolution_convert_fusion.1
  878.3 30.6 %reduce-scatter.8.cloned.1.call-done = bf16[64,512]{1,0:T(8,128)(2,1)} async-done(((bf16[512,512]{1,0:T(8,128)(2,1)}), bf16[64,512]{1,0:T(8,128)(2,1)}) %reduce-scatter.8.cloned.1.call-update) | async-done | bytes 65552 | tf_op jit(solution)/shard_map/reduce_scatter | solution.py:255
  908.9 64.2 %reduce-scatter.14.cloned.1.call-done = bf16[64,512]{1,0:T(8,128)(2,1)} async-done(((bf16[512,512]{1,0:T(8,128)(2,1)}), bf16[64,512]{1,0:T(8,128)(2,1)}) %reduce-scatter.14.cloned.1.call-update) | async-done | bytes 65552 | tf_op jit(solution)/shard_map/reduce_scatter | solution.py:264
  973.1 64.5 %reduce-scatter.10.cloned.1.call-done = bf16[64,512]{1,0:T(8,128)(2,1)} async-done(((bf16[512,512]{1,0:T(8,128)(2,1)}), bf16[64,512]{1,0:T(8,128)(2,1)}) %reduce-scatter.10.cloned.1.call-update) | async-done | bytes 65552 | tf_op jit(solution)/shard_map/reduce_scatter | solution.py:258
  1037.6 64.3 %reduce-scatter.12.cloned.1.call-done = bf16[64,512]{1,0:T(8,128)(2,1)} async-done(((bf16[512,512]{1,0:T(8,128)(2,1)}), bf16[64,512]{1,0:T(8,128)(2,1)}) %reduce-scatter.12.cloned.1.call-update) | async-done | bytes 65552 | tf_op jit(solution)/shard_map/reduce_scatter | solution.py:261
  1101.9 70.6 %reduce-scatter.20.cloned.1.call-done = bf16[256,512]{1,0:T(8,128)(2,1)} async-done(((bf16[2048,512]{1,0:T(8,128)(2,1)}), bf16[256,512]{1,0:T(8,128)(2,1)}) %reduce-scatter.20.cloned.1.call-update) | async-done | bytes 262160 | tf_op jit(solution)/shard_map/reduce_scatter | solution.py:241
  1172.6 70.6 %reduce-scatter.18.cloned.1.call-done = bf16[64,2048]{1,0:T(8,128)(2,1)} async-done(((bf16[512,2048]{1,0:T(8,128)(2,1)}), bf16[64,2048]{1,0:T(8,128)(2,1)}) %reduce-scatter.18.cloned.1.call-update) | async-done | bytes 262160 | tf_op jit(solution)/shard_map/reduce_scatter | solution.py:235
  1246.1 19.6 %all-reduce.12 = (bf16[512]{0:T(512)(128)(2,1)S(1)}, bf16[512]{0:T(512)(128)(2,1)S(1)}, bf16[2048]{0:T(1024)(128)(2,1)S(1)}, bf16[512]{0:T(512)(128)(2,1)S(1)}, ...) all-reduce(bf16[512]{0:T(512)(128)(2,1)S(1)} %get-tuple-element.262, ...), channel_id=7, replica_groups=mesh['rep'=4,'shard'=8] {'shard'}, use_global_device_ids=true, to_apply=%region_32.33.clone | all-reduce | flops 4608 | bytes 18432
  1266.2 5.6 all-reduce.14
  (431 shorter events, 456.9 us)
Async XLA Ops:
  7.2 133.6 %copy-start.29 = (bf16[64,512]{1,0:T(8,128)(2,1)S(1)}, bf16[64,512]{1,0:T(8,128)(2,1)}, u32[]{:S(2)}) copy-start(bf16[64,512]{1,0:T(8,128)(2,1)} %param.28) | copy-start | bytes 196612
  7.2 377.3 %all-gather.4.cloned.1.call-start = ((), (), s32[]{:S(2)}) async-start(), calls=%async_computation.7 | async-start | bytes 2359296 | tf_op jit(solution)/shard_map/all_gather | solution.py:153
  7.9 384.1 %all-gather.6.cloned.1.call-start = ((), (), s32[]{:S(2)}) async-start(), calls=%async_computation.8 | async-start | bytes 2359296 | tf_op jit(solution)/shard_map/all_gather | solution.py:155
  8.0 365.0 %collective-permute-start.4 = (bf16[64,512]{1,0:T(8,128)(2,1)}, bf16[64,512]{1,0:T(8,128)(2,1)S(1)}, u32[]{:S(2)}, u32[]{:S(2)}) collective-permute-start(bf16[64,512]{1,0:T(8,128)(2,1)} %param.29), channel_id=1, source_target_pairs={{0,7},{1,0},{2,1},{3,2},{4,3},{5,4},{6,5},{7,6},{8,15},{9,8},{10,9... | collective-permute-start | bytes 196616 | tf_op jit(solution)/shard_map/ppermute | solution.py:21
  14.0 175.7 %collective-permute-start = (bf16[64,512]{1,0:T(8,128)(2,1)}, bf16[64,512]{1,0:T(8,128)(2,1)S(1)}, u32[]{:S(2)}, u32[]{:S(2)}) collective-permute-start(bf16[64,512]{1,0:T(8,128)(2,1)} %param.29), channel_id=1, source_target_pairs={{0,1},{1,2},{2,3},{3,4},{4,5},{5,6},{6,7},{7,0},{8,9},{9,10},{10,1... | collective-permute-start | bytes 196616 | tf_op jit(solution)/shard_map/ppermute | solution.py:19
  14.1 864.3 %reduce-scatter.16.cloned.1.call-start = ((), (), s32[]{:S(2)}) async-start(), calls=%async_computation.13 | async-start | bytes 589824 | tf_op jit(solution)/shard_map/reduce_scatter | solution.py:267
  42.6 138.9 %copy-start.40 = (f32[512]{0:T(512)}, f32[512]{0:T(512)S(1)}, u32[]{:S(2)}) copy-start(f32[512]{0:T(512)S(1)} %convert_element_type.286) | copy-start | bytes 6148
  42.6 138.9 %copy-start.34 = (f32[512]{0:T(512)}, f32[512]{0:T(512)S(1)}, u32[]{:S(2)}) copy-start(f32[512]{0:T(512)S(1)} %convert_element_type.285) | copy-start | bytes 6148
  75.4 106.2 %copy-start.21 = (bf16[512,512]{1,0:T(8,128)(2,1)}, bf16[512,512]{1,0:T(8,128)(2,1)S(1)}, u32[]{:S(2)}) copy-start(bf16[512,512]{1,0:T(8,128)(2,1)S(1)} %all_gather.47) | copy-start | bytes 1572868
  108.6 67.1 %copy-start.17 = (bf16[512,512]{1,0:T(8,128)(2,1)}, bf16[512,512]{1,0:T(8,128)(2,1)S(1)}, u32[]{:S(2)}) copy-start(bf16[512,512]{1,0:T(8,128)(2,1)S(1)} %all_gather.48) | copy-start | bytes 1572868
  140.8 36.7 %copy-start.19 = (bf16[512,512]{1,0:T(8,128)(2,1)}, bf16[512,512]{1,0:T(8,128)(2,1)S(1)}, u32[]{:S(2)}) copy-start(bf16[512,512]{1,0:T(8,128)(2,1)S(1)} %all_gather.50) | copy-start | bytes 1572868
  174.5 207.7 %copy-start = (bf16[1,1024,512]{1,2,0:T(8,128)(2,1)}, bf16[1,1024,512]{1,2,0:T(8,128)(2,1)S(1)}, u32[]{:S(2)}) copy-start(bf16[1,1024,512]{1,2,0:T(8,128)(2,1)S(1)} %copy.51) | copy-start | bytes 3145732
  174.7 6.8 copy-start.27
  175.6 5.9 copy-start.30
  183.4 2.8 copy-start.23
  189.8 126.6 %collective-permute-start.1 = (bf16[64,512]{1,0:T(8,128)(2,1)S(1)}, bf16[64,512]{1,0:T(8,128)(2,1)S(1)}, u32[]{:S(2)}, u32[]{:S(2)}) collective-permute-start(bf16[64,512]{1,0:T(8,128)(2,1)S(1)} %collective-permute-done), channel_id=1, source_target_pairs={{0,1},{1,2},{2,3},{3,4},{4,5},{5,6},{6,7},{7,0},{8,9},{9,10},{10,1... | collective-permute-start | bytes 196616 | tf_op jit(solution)/shard_map/ppermute | solution.py:19
  190.4 126.6 %copy-start.26 = (bf16[64,512]{1,0:T(8,128)(2,1)S(1)}, bf16[64,512]{1,0:T(8,128)(2,1)}, u32[]{:S(2)}) copy-start(bf16[64,512]{1,0:T(8,128)(2,1)} %param.29) | copy-start | bytes 196612
  190.4 161.2 %copy-start.48 = (bf16[256]{0:T(256)(128)(2,1)S(1)}, bf16[256]{0:T(256)(128)(2,1)}, u32[]{:S(2)}) copy-start(bf16[256]{0:T(256)(128)(2,1)} %param.33) | copy-start | bytes 1540
  190.4 161.3 %copy-start.36 = (s32[1,1024]{1,0:T(1,128)S(1)}, s32[1,1024]{1,0:T(1,128)}, u32[]{:S(2)}) copy-start(s32[1,1024]{1,0:T(1,128)} %param.23) | copy-start | bytes 12292
  316.4 65.7 %copy-start.6 = (bf16[8,1024,64]{1,2,0:T(8,128)(2,1)}, bf16[8,1024,64]{1,2,0:T(8,128)(2,1)S(1)}, u32[]{:S(2)}) copy-start(bf16[8,1024,64]{1,2,0:T(8,128)(2,1)S(1)} %get-tuple-element.167) | copy-start | bytes 3145732
  316.4 56.8 %collective-permute-start.2 = (bf16[64,512]{1,0:T(8,128)(2,1)S(1)}, bf16[64,512]{1,0:T(8,128)(2,1)S(1)}, u32[]{:S(2)}, u32[]{:S(2)}) collective-permute-start(bf16[64,512]{1,0:T(8,128)(2,1)S(1)} %collective-permute-done.1), channel_id=1, source_target_pairs={{0,1},{1,2},{2,3},{3,4},{4,5},{5,6},{6,7},{7,0},{8,9},{9,10},{10,1... | collective-permute-start | bytes 196616 | tf_op jit(solution)/shard_map/ppermute | solution.py:19
  351.6 32.9 %copy-start.42 = (f32[512]{0:T(512)}, f32[512]{0:T(512)S(1)}, u32[]{:S(2)}) copy-start(f32[512]{0:T(512)S(1)} %convert_element_type.298) | copy-start | bytes 6148
  373.0 4.5 collective-permute-start.5
  373.2 7.0 collective-permute-start.3
  377.4 4.6 collective-permute-start.6
  384.5 7.5 copy-start.8
  444.5 7.0 copy-start.25
  444.5 7.0 copy-start.45
  451.5 4.2 copy-start.49
  462.4 3.3 copy-start.7
  467.4 441.6 %reduce-scatter.8.cloned.1.call-start = ((), (), s32[]{:S(2)}) async-start(), calls=%async_computation.9 | async-start | bytes 589824 | tf_op jit(solution)/shard_map/reduce_scatter | solution.py:255
  479.3 363.8 %copy-start.1 = (bf16[1,1024,512]{1,2,0:T(8,128)(2,1)S(1)}, bf16[1,1024,512]{1,2,0:T(8,128)(2,1)}, u32[]{:S(2)}) copy-start(bf16[1,1024,512]{1,2,0:T(8,128)(2,1)} %copy-done) | copy-start | bytes 3145732
  479.3 363.8 %copy-start.28 = (f32[1024]{0:T(1024)S(1)}, f32[1024]{0:T(1024)}, u32[]{:S(2)}) copy-start(f32[1024]{0:T(1024)} %copy-done.27) | copy-start | bytes 12292
  479.3 363.8 %copy-start.31 = (f32[1024]{0:T(1024)S(1)}, f32[1024]{0:T(1024)}, u32[]{:S(2)}) copy-start(f32[1024]{0:T(1024)} %copy-done.30) | copy-start | bytes 12292
  479.3 363.8 %copy-start.35 = (f32[512]{0:T(512)S(1)}, f32[512]{0:T(512)}, u32[]{:S(2)}) copy-start(f32[512]{0:T(512)} %copy-done.34) | copy-start | bytes 6148
  479.3 363.8 %copy-start.41 = (f32[512]{0:T(512)S(1)}, f32[512]{0:T(512)}, u32[]{:S(2)}) copy-start(f32[512]{0:T(512)} %copy-done.40) | copy-start | bytes 6148
  846.0 127.1 %reduce-scatter.14.cloned.1.call-start = ((), (), s32[]{:S(2)}) async-start(), calls=%async_computation.12 | async-start | bytes 589824 | tf_op jit(solution)/shard_map/reduce_scatter | solution.py:264
  848.9 188.7 %reduce-scatter.10.cloned.1.call-start = ((), (), s32[]{:S(2)}) async-start(), calls=%async_computation.10 | async-start | bytes 589824 | tf_op jit(solution)/shard_map/reduce_scatter | solution.py:258
  851.7 250.2 %reduce-scatter.12.cloned.1.call-start = ((), (), s32[]{:S(2)}) async-start(), calls=%async_computation.11 | async-start | bytes 589824 | tf_op jit(solution)/shard_map/reduce_scatter | solution.py:261
  854.6 317.9 %reduce-scatter.20.cloned.1.call-start = ((), (), s32[]{:S(2)}) async-start(), calls=%async_computation.15 | async-start | bytes 2359296 | tf_op jit(solution)/shard_map/reduce_scatter | solution.py:241
  862.0 381.1 %reduce-scatter.18.cloned.1.call-start = ((), (), s32[]{:S(2)}) async-start(), calls=%async_computation.14 | async-start | bytes 2359296 | tf_op jit(solution)/shard_map/reduce_scatter | solution.py:235
  868.7 3.3 copy-start.13
  868.7 413.4 %all-reduce.18.cloned.1.call-start = ((), (), s32[]{:S(2)}) async-start(), calls=%async_computation.16 | async-start | bytes 1703936 | tf_op jit(solution)/shard_map/psum | solution.py:289
  878.2 367.9 %copy-start.37 = (bf16[512]{0:T(512)(128)(2,1)S(1)}, bf16[512]{0:T(512)(128)(2,1)}, u32[]{:S(2)}) copy-start(bf16[512]{0:T(512)(128)(2,1)} %get-tuple-element.260) | copy-start | bytes 3076
  878.2 367.9 %copy-start.38 = (bf16[2048]{0:T(1024)(128)(2,1)S(1)}, bf16[2048]{0:T(1024)(128)(2,1)}, u32[]{:S(2)}) copy-start(bf16[2048]{0:T(1024)(128)(2,1)} %get-tuple-element.346) | copy-start | bytes 12292
  878.3 367.8 %copy-start.39 = (bf16[512]{0:T(512)(128)(2,1)S(1)}, bf16[512]{0:T(512)(128)(2,1)}, u32[]{:S(2)}) copy-start(bf16[512]{0:T(512)(128)(2,1)} %get-tuple-element.330) | copy-start | bytes 3076
  878.3 367.8 %copy-start.44 = (bf16[512]{0:T(512)(128)(2,1)S(1)}, bf16[512]{0:T(512)(128)(2,1)}, u32[]{:S(2)}) copy-start(bf16[512]{0:T(512)(128)(2,1)} %get-tuple-element.348) | copy-start | bytes 3076
  878.3 396.7 %copy-start.3 = (f32[1024,512]{0,1:T(8,128)S(1)}, f32[1024,512]{0,1:T(8,128)}, u32[]{:S(2)}) copy-start(f32[1024,512]{0,1:T(8,128)} %copy-done.2) | copy-start | bytes 6291460
  (26 other events, 41.9 us)
Sparse Core Ops, SparseCore 0:
  10.1 58.4 all-gather.3
  70.8 57.5 all-gather.5
  467.5 62.7 reduce-scatter.15
  846.1 62.7 reduce-scatter.7
  912.1 60.9 reduce-scatter.13
  976.7 60.8 reduce-scatter.9
  1041.0 60.9 reduce-scatter.11
  1105.9 66.6 reduce-scatter.19
  1176.5 66.5 reduce-scatter.17
  1246.1 34.6 all-reduce.17
